TPU v7x, 32 devices: a whole 2x2x4 slice. The times are simulated.
32 devices in a mesh: row: 4 (over y, core), blk: 8 (over z, x).
Axes of the slice: x: 2, y: 2, z: 4, core: 2. Of those that a mesh axis runs over, the one named last changes fastest.
Arguments:
- right_side: float32 [4, 8, 8, 32, 256], P('row', 'blk')
- noise_level: float32 [4, 8, 8, 256], P('row', 'blk'), may hold values from 3 to 6
- near_blocks: bfloat16 [4, 8, 8, 9, 256, 256], P('row', 'blk'), as said below
- skeleton_basis: bfloat16 [4, 8, 8, 64, 256], P('row', 'blk'), may hold values from -0.125 to 0.125
- skeleton_index: int32 [4, 8, 64], P('row', 'blk'), may hold values from 0 to 2047, as said below
- far_list: int32 [4, 8, 7], P('row', 'blk'), may hold values from 0 to 7, as said below
- couplings: bfloat16 [4, 8, 7, 64, 64], P('row', 'blk'), as said below
Outputs:
- solution: float32 [4, 8, 8, 32, 256], P('row', 'blk')
- residual: float32 [4, 8, 8, 32, 256], P('row', 'blk')
- quadratic: float32 [32], replicated
Inputs may be any that keep to these rules, and one draw needn't show every extreme that they name: `far_list`: each device's 7 entries are distinct, none is the device's own blk index, and the two cyclic neighbours along blk are always among them; box b lists box b' exactly when b' lists b, and within a row every box's far boxes lie at the same set of cyclic offsets from its own index. `couplings`: the coupling that box b holds for far box b' is the transpose of the one that b' holds for b. `near_blocks`: A leaf's block for near slot s is the transpose of the block that its slot-s neighbour holds for slot 8 - s; slot 4 blocks are symmetric. `skeleton_index`: each device's 64 entries are distinct tracers of its 2048.
All inputs are finite; a program needn't handle non-finite values.
Results may differ from a plain program's by a relative error of at most 0.03.
Values may be sent and summed in bfloat16 or wider, within the bound.
A program may use at most 64 MiB of HBM per device.

v0:
```python
import jax
import jax.numpy as jnp
from jax import lax
from jax.sharding import PartitionSpec as P

ITERS = 4
LEAF_ROWS = 2
LEAF_COLS = 4


def extended_2(array, sides, width):
    for axis, dim in sides:
        count, length = (lax.axis_size(axis), array.shape[dim])
        up = [(i, (i + 1) % count) for i in range(count)]
        down = [(j, i) for i, j in up]
        last = lax.slice_in_dim(array, length - width, length, axis=dim)
        leading = lax.slice_in_dim(array, 0, width, axis=dim)
        before = lax.ppermute(last, axis, up)
        after = lax.ppermute(leading, axis, down)
        array = jnp.concatenate([before, array, after], axis=dim)
    return array


def local(
    right_side, noise_level, near_blocks, skeleton_basis, skeleton_index, far_list, couplings
):
    local_noise = noise_level[0, 0][:, None, :]
    leaf_count = near_blocks.shape[2]
    width = near_blocks.shape[4]
    blocks_grid = near_blocks[0, 0].reshape(LEAF_ROWS, LEAF_COLS, 9, width, width)
    basis_local = skeleton_basis[0, 0]
    skeleton_local = skeleton_index[0, 0]
    far_local = far_list[0, 0]
    coupling_local = couplings[0, 0]
    points = basis_local.shape[2]
    owner_leaf = skeleton_local // points
    owner_point = skeleton_local % points

    def column_sum(values):
        return jnp.sum(values, axis=(0, 1, 2, 4))

    def residual_sum(values):
        return lax.psum(column_sum(values * values), ("row", "blk"))

    solution = jnp.zeros_like(right_side)
    residual = right_side
    direction = right_side
    norm_now = residual_sum(residual)
    for step_index in range(ITERS):
        rounded = direction.astype(jnp.bfloat16)
        own_field = rounded[0, 0]
        columns = own_field.shape[1]
        leaf_grid = own_field.reshape(LEAF_ROWS, LEAF_COLS, columns, width)
        extended = extended_2(leaf_grid, (("row", 0), ("blk", 1)), 1)
        sources = jnp.stack(
            [
                extended[slot // 3 : slot // 3 + LEAF_ROWS, slot % 3 : slot % 3 + LEAF_COLS]
                for slot in range(9)
            ],
            axis=2,
        )
        near = jnp.einsum(
            "abkci,abkij->abcj", sources, blocks_grid, preferred_element_type=jnp.float32
        )
        result = near.reshape(leaf_count, columns, width)
        picked = own_field[owner_leaf, :, owner_point].astype(jnp.float32)
        skeleton = picked.T + jnp.einsum(
            "lci,lki->ck", own_field, basis_local, preferred_element_type=jnp.float32
        )
        all_skeletons = lax.all_gather(
            skeleton.astype(jnp.bfloat16)[None], "blk", axis=0, tiled=True
        )
        selected = all_skeletons[far_local]
        far_sum = jnp.einsum(
            "jck,jkm->cm", selected, coupling_local, preferred_element_type=jnp.float32
        )
        result = result + jnp.einsum(
            "ck,lki->lci",
            far_sum.astype(jnp.bfloat16),
            basis_local,
            preferred_element_type=jnp.float32,
        )
        result = result.at[owner_leaf, :, owner_point].add(far_sum.T)
        applied = (local_noise * direction[0, 0] + result)[None, None]
        curve = lax.psum(column_sum(direction * applied), ("row", "blk"))
        step_size = norm_now / curve
        solution = solution + step_size[:, None] * direction
        residual = residual - step_size[:, None] * applied
        norm_next = residual_sum(residual)
        direction = residual + (norm_next / norm_now)[:, None] * direction
        norm_now = norm_next
    total = lax.psum(column_sum(right_side * solution), ("row", "blk"))
    tracer_count = (
        lax.axis_size("row") * lax.axis_size("blk") * right_side.shape[2] * right_side.shape[4]
    )
    quadratic = total / tracer_count
    return (solution, residual, quadratic)


def solution(mesh):
    return jax.shard_map(
        local,
        mesh=mesh,
        in_specs=(
            P("row", "blk", None, None, None),
            P("row", "blk", None, None),
            P("row", "blk", None, None, None, None),
            P("row", "blk", None, None, None),
            P("row", "blk", None),
            P("row", "blk", None),
            P("row", "blk", None, None, None),
        ),
        out_specs=(P("row", "blk", None, None, None), P("row", "blk", None, None, None), P()),
        check_vma=False,
    )
```

profile of v0, /device:TPU:0, one launch (start us, length us, event | category | flops | bytes accessed | tf_op | source)
XLA Modules:
  0.0 537.6 jit_solution(16591721626279821936)
XLA Ops:
  1.9 2.5 collective-permute-start.1
  5.8 30.8 %all-gather = bf16[256,64]{1,0:T(8,128)(2,1)S(1)} all-gather(bf16[32,64]{1,0:T(8,128)(2,1)S(1)} %fusion.12), channel_id=2, replica_groups=mesh['row'=4,'blk'=8] {'blk'}, dimensions={0}, use_global_device_ids=true | all-gather | bytes 36864 | tf_op jit(solution)/shard_map/all_gather | solution.py:70
  37.3 4.2 collective-permute-start.3
  43.5 5.1 collective-permute-done.2
  48.8 5.4 %fusion.95 = f32[2,4,32,256,1]{3,2,4,1,0:T(8,128)S(1)} fusion(bf16[2,4,9,32,256]{4,3,2,1,0:T(8,128)(2,1)S(1)} %fusion.58, bf16[2,4,9,256,256]{4,3,2,1,0:T(8,128)(2,1)} %bitcast.461), kind=kOutput, calls=%fused_computation.214 | convolution fusion | flops 301989888 | bytes 10878976 | tf_op jit(solution)/shard_map/abkci,abkij->abcj/dot_general | solution.py:62
  54.7 3.7 scatter_fusion
  59.0 36.9 %all-reduce = (f32[32]{0:T(128)S(1)}, f32[32]{0:T(128)S(1)}) all-reduce(f32[32]{0:T(128)S(1)} %get-tuple-element.32, f32[32]{0:T(128)S(1)} %fusion.16), channel_id=1, replica_groups=mesh['row'=4,'blk'=8] {'row','blk'}, use_global_device_ids=true, to_apply=%region_1.2 | all-reduce | flops 64 | bytes 512 | tf_op jit(solution)/shard_map/psum | solution.py:43
  96.1 42.0 %psum.65 = f32[32]{0:T(128)S(1)} all-reduce(f32[32]{0:T(128)S(1)} %multiply_reduce_fusion.3), channel_id=1, replica_groups=mesh['row'=4,'blk'=8] {'row','blk'}, use_global_device_ids=true, to_apply=%region_6.7 | all-reduce | flops 32 | bytes 256 | tf_op jit(solution)/shard_map/psum | solution.py:43
  140.2 30.6 %all-gather.1 = bf16[256,64]{1,0:T(8,128)(2,1)S(1)} all-gather(bf16[32,64]{1,0:T(8,128)(2,1)S(1)} %fusion.13), channel_id=3, replica_groups=mesh['row'=4,'blk'=8] {'blk'}, dimensions={0}, use_global_device_ids=true | all-gather | bytes 36864 | tf_op jit(solution)/shard_map/all_gather | solution.py:70
  171.4 3.2 collective-permute-start.7
  174.9 1.6 collective-permute-done.7
  176.5 5.1 collective-permute-done.6
  181.8 5.4 %fusion.96 = f32[2,4,32,256,1]{3,2,4,1,0:T(8,128)S(1)} fusion(bf16[2,4,9,32,256]{4,3,2,1,0:T(8,128)(2,1)S(1)} %fusion.48, bf16[2,4,9,256,256]{4,3,2,1,0:T(8,128)(2,1)} %bitcast.462), kind=kOutput, calls=%fused_computation.215 | convolution fusion | flops 301989888 | bytes 10878976 | tf_op jit(solution)/shard_map/abkci,abkij->abcj/dot_general | solution.py:62
  187.7 3.7 scatter_fusion.1
  191.8 36.9 %psum.66 = f32[32]{0:T(128)S(1)} all-reduce(f32[32]{0:T(128)S(1)} %fusion.19), channel_id=1, replica_groups=mesh['row'=4,'blk'=8] {'row','blk'}, use_global_device_ids=true, to_apply=%region_9.10 | all-reduce | flops 32 | bytes 256 | tf_op jit(solution)/shard_map/psum | solution.py:85
  229.0 41.7 %psum.67 = f32[32]{0:T(128)S(1)} all-reduce(f32[32]{0:T(128)S(1)} %get-tuple-element.13), channel_id=1, replica_groups=mesh['row'=4,'blk'=8] {'row','blk'}, use_global_device_ids=true, to_apply=%region_11.12 | all-reduce | flops 32 | bytes 256 | tf_op jit(solution)/shard_map/psum | solution.py:43
  272.9 30.5 %all-gather.2 = bf16[256,64]{1,0:T(8,128)(2,1)S(1)} all-gather(bf16[32,64]{1,0:T(8,128)(2,1)S(1)} %fusion.14), channel_id=4, replica_groups=mesh['row'=4,'blk'=8] {'blk'}, dimensions={0}, use_global_device_ids=true | all-gather | bytes 36864 | tf_op jit(solution)/shard_map/all_gather | solution.py:70
  304.1 3.2 collective-permute-start.11
  307.5 1.6 collective-permute-done.11
  309.2 5.1 collective-permute-done.10
  314.5 5.4 %fusion.97 = f32[2,4,32,256,1]{3,2,4,1,0:T(8,128)S(1)} fusion(bf16[2,4,9,32,256]{4,3,2,1,0:T(8,128)(2,1)S(1)} %fusion.38, bf16[2,4,9,256,256]{4,3,2,1,0:T(8,128)(2,1)} %bitcast.463), kind=kOutput, calls=%fused_computation.216 | convolution fusion | flops 301989888 | bytes 10878976 | tf_op jit(solution)/shard_map/abkci,abkij->abcj/dot_general | solution.py:62
  320.4 3.7 scatter_fusion.2
  324.5 36.9 %psum.68 = f32[32]{0:T(128)S(1)} all-reduce(f32[32]{0:T(128)S(1)} %fusion.18), channel_id=1, replica_groups=mesh['row'=4,'blk'=8] {'row','blk'}, use_global_device_ids=true, to_apply=%region_14.15 | all-reduce | flops 32 | bytes 256 | tf_op jit(solution)/shard_map/psum | solution.py:85
  361.6 42.0 %psum.69 = f32[32]{0:T(128)S(1)} all-reduce(f32[32]{0:T(128)S(1)} %get-tuple-element.9), channel_id=1, replica_groups=mesh['row'=4,'blk'=8] {'row','blk'}, use_global_device_ids=true, to_apply=%region_16.17 | all-reduce | flops 32 | bytes 256 | tf_op jit(solution)/shard_map/psum | solution.py:43
  405.7 30.6 %all-gather.3 = bf16[256,64]{1,0:T(8,128)(2,1)S(1)} all-gather(bf16[32,64]{1,0:T(8,128)(2,1)S(1)} %fusion.15), channel_id=5, replica_groups=mesh['row'=4,'blk'=8] {'blk'}, dimensions={0}, use_global_device_ids=true | all-gather | bytes 36864 | tf_op jit(solution)/shard_map/all_gather | solution.py:70
  436.9 3.2 collective-permute-start.15
  440.4 1.6 collective-permute-done.15
  442.0 5.1 collective-permute-done.14
  447.3 5.4 %fusion.98 = f32[2,4,32,256,1]{3,2,4,1,0:T(8,128)S(1)} fusion(bf16[2,4,9,32,256]{4,3,2,1,0:T(8,128)(2,1)S(1)} %fusion.28, bf16[2,4,9,256,256]{4,3,2,1,0:T(8,128)(2,1)} %bitcast.464), kind=kOutput, calls=%fused_computation.217 | convolution fusion | flops 301989888 | bytes 10878976 | tf_op jit(solution)/shard_map/abkci,abkij->abcj/dot_general | solution.py:62
  453.3 3.7 scatter_fusion.3
  457.4 36.9 %psum.70 = f32[32]{0:T(128)S(1)} all-reduce(f32[32]{0:T(128)S(1)} %fusion.17), channel_id=1, replica_groups=mesh['row'=4,'blk'=8] {'row','blk'}, use_global_device_ids=true, to_apply=%region_19.20 | all-reduce | flops 32 | bytes 256 | tf_op jit(solution)/shard_map/psum | solution.py:85
  495.3 41.7 %psum.71 = f32[32]{0:T(128)S(1)} all-reduce(f32[32]{0:T(128)S(1)} %get-tuple-element.5), channel_id=1, replica_groups=mesh['row'=4,'blk'=8] {'row','blk'}, use_global_device_ids=true, to_apply=%region_21.22 | all-reduce | flops 32 | bytes 256 | tf_op jit(solution)/shard_map/psum | solution.py:92
  (145 shorter events, 20.9 us)
Async XLA Ops:
  0.6 5.0 copy-start
  0.6 4.0 copy-start.4
  0.7 36.0 %copy-start.5 = (s32[1,1,7]{2,1,0:T(1,128)S(1)}, s32[1,1,7]{2,1,0:T(1,128)}, u32[]{:S(2)}) copy-start(s32[1,1,7]{2,1,0:T(1,128)} %param.12) | copy-start | bytes 88
  0.7 40.9 %copy-start.2 = (bf16[1,1,7,64,64]{4,3,2,1,0:T(8,128)(2,1)S(1)}, bf16[1,1,7,64,64]{4,3,2,1,0:T(8,128)(2,1)}, u32[]{:S(2)}) copy-start(bf16[1,1,7,64,64]{4,3,2,1,0:T(8,128)(2,1)} %param.13) | copy-start | bytes 172036
  1.9 39.9 %copy-start.1 = (f32[1,1,8,32,256]{4,3,2,1,0:T(8,128)S(1)}, f32[1,1,8,32,256]{4,3,2,1,0:T(8,128)}, u32[]{:S(2)}) copy-start(f32[1,1,8,32,256]{4,3,2,1,0:T(8,128)} %param.7) | copy-start | bytes 786436
  1.9 35.3 %collective-permute-start.1 = (bf16[1,4,32,256]{3,2,1,0:T(8,128)(2,1)S(1)}, bf16[1,4,32,256]{3,2,1,0:T(8,128)(2,1)S(1)}, u32[]{:S(2)}, u32[]{:S(2)}) collective-permute-start(bf16[1,4,32,256]{3,2,1,0:T(8,128)(2,1)S(1)} %get-tuple-element.45), channel_id=1, source_target_pairs={{8,0},{16,8},{24,16},{0,24},{9,1},{17,9},{25,17},{1,25},{10,2},{18... | collective-permute-start | bytes 196616 | tf_op jit(solution)/shard_map/ppermute | solution.py:19
  4.4 32.9 %collective-permute-start = (bf16[1,4,32,256]{3,2,1,0:T(8,128)(2,1)S(1)}, bf16[1,4,32,256]{3,2,1,0:T(8,128)(2,1)S(1)}, u32[]{:S(2)}, u32[]{:S(2)}) collective-permute-start(bf16[1,4,32,256]{3,2,1,0:T(8,128)(2,1)S(1)} %get-tuple-element.44), channel_id=1, source_target_pairs={{0,8},{8,16},{16,24},{24,0},{1,9},{9,17},{17,25},{25,1},{2,10},{10... | collective-permute-start | bytes 196616 | tf_op jit(solution)/shard_map/ppermute | solution.py:18
  37.3 6.1 %collective-permute-start.3 = (bf16[4,1,32,256]{3,2,1,0:T(8,128)(2,1)S(1)}, bf16[4,1,32,256]{3,2,1,0:T(8,128)(2,1)S(1)}, u32[]{:S(2)}, u32[]{:S(2)}) collective-permute-start(bf16[4,1,32,256]{3,2,1,0:T(8,128)(2,1)S(1)} %get-tuple-element.36), channel_id=1, source_target_pairs={{1,0},{2,1},{3,2},{4,3},{5,4},{6,5},{7,6},{0,7},{9,8},{10,9},{11,1... | collective-permute-start | bytes 196616 | tf_op jit(solution)/shard_map/ppermute | solution.py:19
  41.5 7.0 %collective-permute-start.2 = (bf16[4,1,32,256]{3,2,1,0:T(8,128)(2,1)S(1)}, bf16[4,1,32,256]{3,2,1,0:T(8,128)(2,1)S(1)}, u32[]{:S(2)}, u32[]{:S(2)}) collective-permute-start(bf16[4,1,32,256]{3,2,1,0:T(8,128)(2,1)S(1)} %get-tuple-element.37), channel_id=1, source_target_pairs={{0,1},{1,2},{2,3},{3,4},{4,5},{5,6},{6,7},{7,0},{8,9},{9,10},{10,1... | collective-permute-start | bytes 196616 | tf_op jit(solution)/shard_map/ppermute | solution.py:18
  48.7 5.4 %copy-start.3 = (f32[1,1,8,256]{3,2,1,0:T(8,128)S(1)}, f32[1,1,8,256]{3,2,1,0:T(8,128)}, u32[]{:S(2)}) copy-start(f32[1,1,8,256]{3,2,1,0:T(8,128)} %param.8) | copy-start | bytes 24580
  138.2 33.1 %collective-permute-start.5 = (bf16[1,4,32,256]{3,2,1,0:T(8,128)(2,1)S(1)}, bf16[1,4,32,256]{3,2,1,0:T(8,128)(2,1)S(1)}, u32[]{:S(2)}, u32[]{:S(2)}) collective-permute-start(bf16[1,4,32,256]{3,2,1,0:T(8,128)(2,1)S(1)} %get-tuple-element.43), channel_id=1, source_target_pairs={{8,0},{16,8},{24,16},{0,24},{9,1},{17,9},{25,17},{1,25},{10,2},{18... | collective-permute-start | bytes 196616 | tf_op jit(solution)/shard_map/ppermute | solution.py:19
  138.6 32.7 %collective-permute-start.4 = (bf16[1,4,32,256]{3,2,1,0:T(8,128)(2,1)S(1)}, bf16[1,4,32,256]{3,2,1,0:T(8,128)(2,1)S(1)}, u32[]{:S(2)}, u32[]{:S(2)}) collective-permute-start(bf16[1,4,32,256]{3,2,1,0:T(8,128)(2,1)S(1)} %get-tuple-element.42), channel_id=1, source_target_pairs={{0,8},{8,16},{16,24},{24,0},{1,9},{9,17},{17,25},{25,1},{2,10},{10... | collective-permute-start | bytes 196616 | tf_op jit(solution)/shard_map/ppermute | solution.py:18
  171.4 5.2 collective-permute-start.7
  174.6 7.0 %collective-permute-start.6 = (bf16[4,1,32,256]{3,2,1,0:T(8,128)(2,1)S(1)}, bf16[4,1,32,256]{3,2,1,0:T(8,128)(2,1)S(1)}, u32[]{:S(2)}, u32[]{:S(2)}) collective-permute-start(bf16[4,1,32,256]{3,2,1,0:T(8,128)(2,1)S(1)} %get-tuple-element.31), channel_id=1, source_target_pairs={{0,1},{1,2},{2,3},{3,4},{4,5},{5,6},{6,7},{7,0},{8,9},{9,10},{10,1... | collective-permute-start | bytes 196616 | tf_op jit(solution)/shard_map/ppermute | solution.py:18
  270.8 33.2 %collective-permute-start.9 = (bf16[1,4,32,256]{3,2,1,0:T(8,128)(2,1)S(1)}, bf16[1,4,32,256]{3,2,1,0:T(8,128)(2,1)S(1)}, u32[]{:S(2)}, u32[]{:S(2)}) collective-permute-start(bf16[1,4,32,256]{3,2,1,0:T(8,128)(2,1)S(1)} %get-tuple-element.41), channel_id=1, source_target_pairs={{8,0},{16,8},{24,16},{0,24},{9,1},{17,9},{25,17},{1,25},{10,2},{18... | collective-permute-start | bytes 196616 | tf_op jit(solution)/shard_map/ppermute | solution.py:19
  271.5 32.5 %collective-permute-start.8 = (bf16[1,4,32,256]{3,2,1,0:T(8,128)(2,1)S(1)}, bf16[1,4,32,256]{3,2,1,0:T(8,128)(2,1)S(1)}, u32[]{:S(2)}, u32[]{:S(2)}) collective-permute-start(bf16[1,4,32,256]{3,2,1,0:T(8,128)(2,1)S(1)} %get-tuple-element.40), channel_id=1, source_target_pairs={{0,8},{8,16},{16,24},{24,0},{1,9},{9,17},{17,25},{25,1},{2,10},{10... | collective-permute-start | bytes 196616 | tf_op jit(solution)/shard_map/ppermute | solution.py:18
  304.1 5.1 collective-permute-start.11
  307.3 7.0 %collective-permute-start.10 = (bf16[4,1,32,256]{3,2,1,0:T(8,128)(2,1)S(1)}, bf16[4,1,32,256]{3,2,1,0:T(8,128)(2,1)S(1)}, u32[]{:S(2)}, u32[]{:S(2)}) collective-permute-start(bf16[4,1,32,256]{3,2,1,0:T(8,128)(2,1)S(1)} %get-tuple-element.27), channel_id=1, source_target_pairs={{0,1},{1,2},{2,3},{3,4},{4,5},{5,6},{6,7},{7,0},{8,9},{9,10},{10,1... | collective-permute-start | bytes 196616 | tf_op jit(solution)/shard_map/ppermute | solution.py:18
  403.7 33.1 %collective-permute-start.13 = (bf16[1,4,32,256]{3,2,1,0:T(8,128)(2,1)S(1)}, bf16[1,4,32,256]{3,2,1,0:T(8,128)(2,1)S(1)}, u32[]{:S(2)}, u32[]{:S(2)}) collective-permute-start(bf16[1,4,32,256]{3,2,1,0:T(8,128)(2,1)S(1)} %get-tuple-element.39), channel_id=1, source_target_pairs={{8,0},{16,8},{24,16},{0,24},{9,1},{17,9},{25,17},{1,25},{10,2},{18... | collective-permute-start | bytes 196616 | tf_op jit(solution)/shard_map/ppermute | solution.py:19
  404.1 32.8 %collective-permute-start.12 = (bf16[1,4,32,256]{3,2,1,0:T(8,128)(2,1)S(1)}, bf16[1,4,32,256]{3,2,1,0:T(8,128)(2,1)S(1)}, u32[]{:S(2)}, u32[]{:S(2)}) collective-permute-start(bf16[1,4,32,256]{3,2,1,0:T(8,128)(2,1)S(1)} %get-tuple-element.38), channel_id=1, source_target_pairs={{0,8},{8,16},{16,24},{24,0},{1,9},{9,17},{17,25},{25,1},{2,10},{10... | collective-permute-start | bytes 196616 | tf_op jit(solution)/shard_map/ppermute | solution.py:18
  436.9 5.1 collective-permute-start.15
  440.1 7.0 %collective-permute-start.14 = (bf16[4,1,32,256]{3,2,1,0:T(8,128)(2,1)S(1)}, bf16[4,1,32,256]{3,2,1,0:T(8,128)(2,1)S(1)}, u32[]{:S(2)}, u32[]{:S(2)}) collective-permute-start(bf16[4,1,32,256]{3,2,1,0:T(8,128)(2,1)S(1)} %get-tuple-element.23), channel_id=1, source_target_pairs={{0,1},{1,2},{2,3},{3,4},{4,5},{5,6},{6,7},{7,0},{8,9},{9,10},{10,1... | collective-permute-start | bytes 196616 | tf_op jit(solution)/shard_map/ppermute | solution.py:18
where the time goes:
time: 539 us; the launch traced here: 538 us
  blocking collectives  438 us (81%)
  waiting for transfers between devices  26.4 us (5%)
  matrix products  23.9 us (4%)
  other arithmetic  19.6 us (4%)
  starting transfers between devices  18.2 us (3%)
  local copies, waits for them, and re-layouts  10.6 us (2%)
    psum x4, blocking collectives, residual_sum(): return lax.psum(column_sum(values * values), ('row', 'blk'))  163 us
    all_gather x4, blocking collectives, local(): lax.all_gather(skeleton.astype(jnp.bfloat16)[None], 'blk', axis=0, tiled=...  123 us
    psum x3, blocking collectives, local(): curve = lax.psum(column_sum(direction * applied), ('row', 'blk'))  111 us
    psum x1, blocking collectives, local(): total = lax.psum(column_sum(right_side * solution), ('row', 'blk'))  41.7 us
    dot_general x4, matrix products, local(): jnp.einsum('abkci,abkij->abcj', sources, blocks_grid, preferred_element_t...  21.6 us
    ppermute x8, waiting for transfers between devices, extended_2(): before = lax.ppermute(last, axis, up)  20.2 us
    ppermute x8, starting transfers between devices, extended_2(): after = lax.ppermute(leading, axis, down)  17.8 us
    scatter-add x4, other arithmetic, local(): result = result.at[owner_leaf, :, owner_point].add(far_sum.T)  14.7 us
  transfers between devices with their start and end apart: 16, of which 8 were waited for; matrix products, arithmetic and copies ran while one was open for 2% of the time, Pallas kernels for 0%

commit v1 on v0

--- a/solution.py
+++ b/solution.py
@@ -6,6 +6,24 @@
 ITERS = 4
 LEAF_ROWS = 2
 LEAF_COLS = 4
+
+
+def joined_along(parts, dim):
+    shape = list(parts.shape[1:])
+    shape[dim] *= parts.shape[0]
+    return jnp.moveaxis(parts, 0, dim).reshape(shape)
+
+
+def doubled(array, axis):
+    size = lax.axis_size(axis)
+    blocks = array[None]
+    for level in range(size.bit_length() - 1):
+        bit = 1 << level
+        theirs = lax.ppermute(blocks, axis, [(i, i ^ bit) for i in range(size)])
+        both = jnp.stack([blocks, theirs])
+        upper = lax.axis_index(axis) >> level & 1
+        blocks = jnp.where(upper == 0, both, both[::-1]).reshape(-1, *array.shape)
+    return blocks
 
 
 def extended_2(array, sides, width):
@@ -67,9 +85,8 @@
         skeleton = picked.T + jnp.einsum(
             "lci,lki->ck", own_field, basis_local, preferred_element_type=jnp.float32
         )
-        all_skeletons = lax.all_gather(
-            skeleton.astype(jnp.bfloat16)[None], "blk", axis=0, tiled=True
-        )
+        x = skeleton.astype(jnp.bfloat16)[None]
+        all_skeletons = joined_along(doubled(x, "blk"), 0)
         selected = all_skeletons[far_local]
         far_sum = jnp.einsum(
             "jck,jkm->cm", selected, coupling_local, preferred_element_type=jnp.float32

time: 539 us -> 465 us (0.86)
  blocking collectives: 438 us -> 315 us
  waiting for transfers between devices: 26.4 us -> 59.4 us
  starting transfers between devices: 18.2 us -> 32.9 us
    all_gather x4 -> x0, blocking collectives: 123 us -> none  [local(): lax.all_gather(skeleton.astype(jnp.bfloat16)[None], 'blk', axis=0, tiled=...]
    ppermute x0 -> x12, waiting for transfers between devices: none -> 32.6 us  [doubled(): theirs = lax.ppermute(blocks, axis, [(i, i ^ bit) for i in range(size)])]
    ppermute x0 -> x12, starting transfers between devices: none -> 16 us  [doubled(): theirs = lax.ppermute(blocks, axis, [(i, i ^ bit) for i in range(size)])]
  transfers between devices with their start and end apart: 16 -> 28, of which waited for: 8 -> 20; matrix products, arithmetic and copies ran while one was open for 2% -> 1% of each run, Pallas kernels for 0% -> 0%
where the time goes in v1:
time: 465 us; the launch traced here: 464 us
  blocking collectives  315 us (68%)
  waiting for transfers between devices  59.4 us (13%)
  starting transfers between devices  32.9 us (7%)
  matrix products  23.9 us (5%)
  other arithmetic  20.6 us (4%)
  local copies, waits for them, and re-layouts  10.6 us (2%)
    psum x4, blocking collectives, residual_sum(): return lax.psum(column_sum(values * values), ('row', 'blk'))  163 us
    psum x3, blocking collectives, local(): curve = lax.psum(column_sum(direction * applied), ('row', 'blk'))  111 us
    psum x1, blocking collectives, local(): total = lax.psum(column_sum(right_side * solution), ('row', 'blk'))  41.1 us
    ppermute x12, waiting for transfers between devices, doubled(): theirs = lax.ppermute(blocks, axis, [(i, i ^ bit) for i in range(size)])  32.6 us
    dot_general x4, matrix products, local(): jnp.einsum('abkci,abkij->abcj', sources, blocks_grid, preferred_element_t...  21.6 us
    ppermute x8, waiting for transfers between devices, extended_2(): before = lax.ppermute(last, axis, up)  20.2 us
    ppermute x12, starting transfers between devices, doubled(): theirs = lax.ppermute(blocks, axis, [(i, i ^ bit) for i in range(size)])  16 us
    ppermute x8, starting transfers between devices, extended_2(): after = lax.ppermute(leading, axis, down)  15.4 us
  transfers between devices with their start and end apart: 28, of which 20 were waited for; matrix products, arithmetic and copies ran while one was open for 1% of the time, Pallas kernels for 0%

profile of v1, /device:TPU:0, one launch (start us, length us, event | category | flops | bytes accessed | tf_op | source)
XLA Modules:
  0.0 463.9 jit_solution(14017042333605788116)
XLA Ops:
  4.0 3.0 collective-permute-start.4
  12.6 3.1 collective-permute-start.6
  18.2 5.1 %collective-permute-start.3 = (bf16[4,1,32,256]{3,2,1,0:T(8,128)(2,1)S(1)}, bf16[4,1,32,256]{3,2,1,0:T(8,128)(2,1)S(1)}, u32[]{:S(2)}, u32[]{:S(2)}) collective-permute-start(bf16[4,1,32,256]{3,2,1,0:T(8,128)(2,1)S(1)} %get-tuple-element.36), channel_id=1, source_target_pairs={{1,0},{2,1},{3,2},{4,3},{5,4},{6,5},{7,6},{0,7},{9,8},{10,9},{11,1... | collective-permute-start | bytes 196616 | tf_op jit(solution)/shard_map/ppermute | solution.py:37
  25.3 5.1 %collective-permute-done.2 = bf16[4,1,32,256]{3,2,1,0:T(8,128)(2,1)S(1)} collective-permute-done((bf16[4,1,32,256]{3,2,1,0:T(8,128)(2,1)S(1)}, bf16[4,1,32,256]{3,2,1,0:T(8,128)(2,1)S(1)}, u32[]{:S(2)}, u32[]{:S(2)}) %collective-permute-start.2) | collective-permute-done | bytes 65568 | tf_op jit(solution)/shard_map/ppermute | solution.py:36
  30.6 5.4 %fusion.103 = f32[2,4,32,256,1]{3,2,4,1,0:T(8,128)S(1)} fusion(bf16[2,4,9,32,256]{4,3,2,1,0:T(8,128)(2,1)S(1)} %fusion.58, bf16[2,4,9,256,256]{4,3,2,1,0:T(8,128)(2,1)} %bitcast.517), kind=kOutput, calls=%fused_computation.246 | convolution fusion | flops 301989888 | bytes 10878976 | tf_op jit(solution)/shard_map/abkci,abkij->abcj/dot_general | solution.py:80
  36.5 3.7 scatter_fusion
  40.8 36.9 %all-reduce = (f32[32]{0:T(128)S(1)}, f32[32]{0:T(128)S(1)}) all-reduce(f32[32]{0:T(128)S(1)} %get-tuple-element.32, f32[32]{0:T(128)S(1)} %fusion.16), channel_id=1, replica_groups=mesh['row'=4,'blk'=8] {'row','blk'}, use_global_device_ids=true, to_apply=%region_1.2 | all-reduce | flops 64 | bytes 512 | tf_op jit(solution)/shard_map/psum | solution.py:61
  77.9 42.4 %psum.65 = f32[32]{0:T(128)S(1)} all-reduce(f32[32]{0:T(128)S(1)} %multiply_reduce_fusion.3), channel_id=1, replica_groups=mesh['row'=4,'blk'=8] {'row','blk'}, use_global_device_ids=true, to_apply=%region_6.7 | all-reduce | flops 32 | bytes 256 | tf_op jit(solution)/shard_map/psum | solution.py:61
  125.9 3.7 collective-permute-done.12
  130.4 4.1 collective-permute-done.13
  135.2 3.2 collective-permute-start.10
  140.3 5.1 %collective-permute-done.9 = bf16[4,1,32,256]{3,2,1,0:T(8,128)(2,1)S(1)} collective-permute-done((bf16[4,1,32,256]{3,2,1,0:T(8,128)(2,1)S(1)}, bf16[4,1,32,256]{3,2,1,0:T(8,128)(2,1)S(1)}, u32[]{:S(2)}, u32[]{:S(2)}) %collective-permute-start.9) | collective-permute-done | bytes 65568 | tf_op jit(solution)/shard_map/ppermute | solution.py:36
  145.6 5.4 %fusion.104 = f32[2,4,32,256,1]{3,2,4,1,0:T(8,128)S(1)} fusion(bf16[2,4,9,32,256]{4,3,2,1,0:T(8,128)(2,1)S(1)} %fusion.48, bf16[2,4,9,256,256]{4,3,2,1,0:T(8,128)(2,1)} %bitcast.518), kind=kOutput, calls=%fused_computation.247 | convolution fusion | flops 301989888 | bytes 10878976 | tf_op jit(solution)/shard_map/abkci,abkij->abcj/dot_general | solution.py:80
  151.5 3.7 scatter_fusion.1
  155.6 36.9 %psum.66 = f32[32]{0:T(128)S(1)} all-reduce(f32[32]{0:T(128)S(1)} %fusion.19), channel_id=1, replica_groups=mesh['row'=4,'blk'=8] {'row','blk'}, use_global_device_ids=true, to_apply=%region_9.10 | all-reduce | flops 32 | bytes 256 | tf_op jit(solution)/shard_map/psum | solution.py:102
  192.7 41.4 %psum.67 = f32[32]{0:T(128)S(1)} all-reduce(f32[32]{0:T(128)S(1)} %get-tuple-element.13), channel_id=1, replica_groups=mesh['row'=4,'blk'=8] {'row','blk'}, use_global_device_ids=true, to_apply=%region_11.12 | all-reduce | flops 32 | bytes 256 | tf_op jit(solution)/shard_map/psum | solution.py:61
  239.8 3.7 collective-permute-done.19
  244.3 4.1 collective-permute-done.20
  249.1 3.1 collective-permute-start.17
  254.0 5.1 %collective-permute-done.16 = bf16[4,1,32,256]{3,2,1,0:T(8,128)(2,1)S(1)} collective-permute-done((bf16[4,1,32,256]{3,2,1,0:T(8,128)(2,1)S(1)}, bf16[4,1,32,256]{3,2,1,0:T(8,128)(2,1)S(1)}, u32[]{:S(2)}, u32[]{:S(2)}) %collective-permute-start.16) | collective-permute-done | bytes 65568 | tf_op jit(solution)/shard_map/ppermute | solution.py:36
  259.3 5.4 %fusion.105 = f32[2,4,32,256,1]{3,2,4,1,0:T(8,128)S(1)} fusion(bf16[2,4,9,32,256]{4,3,2,1,0:T(8,128)(2,1)S(1)} %fusion.38, bf16[2,4,9,256,256]{4,3,2,1,0:T(8,128)(2,1)} %bitcast.519), kind=kOutput, calls=%fused_computation.248 | convolution fusion | flops 301989888 | bytes 10878976 | tf_op jit(solution)/shard_map/abkci,abkij->abcj/dot_general | solution.py:80
  265.3 3.7 scatter_fusion.2
  269.4 36.9 %psum.68 = f32[32]{0:T(128)S(1)} all-reduce(f32[32]{0:T(128)S(1)} %fusion.18), channel_id=1, replica_groups=mesh['row'=4,'blk'=8] {'row','blk'}, use_global_device_ids=true, to_apply=%region_14.15 | all-reduce | flops 32 | bytes 256 | tf_op jit(solution)/shard_map/psum | solution.py:102
  306.5 42.5 %psum.69 = f32[32]{0:T(128)S(1)} all-reduce(f32[32]{0:T(128)S(1)} %get-tuple-element.9), channel_id=1, replica_groups=mesh['row'=4,'blk'=8] {'row','blk'}, use_global_device_ids=true, to_apply=%region_16.17 | all-reduce | flops 32 | bytes 256 | tf_op jit(solution)/shard_map/psum | solution.py:61
  354.7 3.7 collective-permute-done.26
  359.2 4.1 collective-permute-done.27
  364.0 3.1 collective-permute-start.24
  369.0 5.1 %collective-permute-done.23 = bf16[4,1,32,256]{3,2,1,0:T(8,128)(2,1)S(1)} collective-permute-done((bf16[4,1,32,256]{3,2,1,0:T(8,128)(2,1)S(1)}, bf16[4,1,32,256]{3,2,1,0:T(8,128)(2,1)S(1)}, u32[]{:S(2)}, u32[]{:S(2)}) %collective-permute-start.23) | collective-permute-done | bytes 65568 | tf_op jit(solution)/shard_map/ppermute | solution.py:36
  374.3 5.4 %fusion.106 = f32[2,4,32,256,1]{3,2,4,1,0:T(8,128)S(1)} fusion(bf16[2,4,9,32,256]{4,3,2,1,0:T(8,128)(2,1)S(1)} %fusion.28, bf16[2,4,9,256,256]{4,3,2,1,0:T(8,128)(2,1)} %bitcast.520), kind=kOutput, calls=%fused_computation.249 | convolution fusion | flops 301989888 | bytes 10878976 | tf_op jit(solution)/shard_map/abkci,abkij->abcj/dot_general | solution.py:80
  380.2 3.7 scatter_fusion.3
  384.3 36.9 %psum.70 = f32[32]{0:T(128)S(1)} all-reduce(f32[32]{0:T(128)S(1)} %fusion.17), channel_id=1, replica_groups=mesh['row'=4,'blk'=8] {'row','blk'}, use_global_device_ids=true, to_apply=%region_19.20 | all-reduce | flops 32 | bytes 256 | tf_op jit(solution)/shard_map/psum | solution.py:102
  422.2 41.1 %psum.71 = f32[32]{0:T(128)S(1)} all-reduce(f32[32]{0:T(128)S(1)} %get-tuple-element.5), channel_id=1, replica_groups=mesh['row'=4,'blk'=8] {'row','blk'}, use_global_device_ids=true, to_apply=%region_21.22 | all-reduce | flops 32 | bytes 256 | tf_op jit(solution)/shard_map/psum | solution.py:109
  (187 shorter events, 46.6 us)
Async XLA Ops:
  0.6 15.0 %copy-start.1 = (f32[1,1,8,32,256]{4,3,2,1,0:T(8,128)S(1)}, f32[1,1,8,32,256]{4,3,2,1,0:T(8,128)}, u32[]{:S(2)}) copy-start(f32[1,1,8,32,256]{4,3,2,1,0:T(8,128)} %param.7) | copy-start | bytes 786436
  0.7 10.2 %copy-start.4 = (s32[1,1,7]{2,1,0:T(1,128)S(1)}, s32[1,1,7]{2,1,0:T(1,128)}, u32[]{:S(2)}) copy-start(s32[1,1,7]{2,1,0:T(1,128)} %param.12) | copy-start | bytes 88
  4.0 4.6 collective-permute-start.4
  7.0 16.4 %copy-start.2 = (bf16[1,1,7,64,64]{4,3,2,1,0:T(8,128)(2,1)S(1)}, bf16[1,1,7,64,64]{4,3,2,1,0:T(8,128)(2,1)}, u32[]{:S(2)}) copy-start(bf16[1,1,7,64,64]{4,3,2,1,0:T(8,128)(2,1)} %param.13) | copy-start | bytes 172036
  7.0 11.2 %collective-permute-start.1 = (bf16[1,4,32,256]{3,2,1,0:T(8,128)(2,1)S(1)}, bf16[1,4,32,256]{3,2,1,0:T(8,128)(2,1)S(1)}, u32[]{:S(2)}, u32[]{:S(2)}) collective-permute-start(bf16[1,4,32,256]{3,2,1,0:T(8,128)(2,1)S(1)} %get-tuple-element.45), channel_id=1, source_target_pairs={{8,0},{16,8},{24,16},{0,24},{9,1},{17,9},{25,17},{1,25},{10,2},{18... | collective-permute-start | bytes 196616 | tf_op jit(solution)/shard_map/ppermute | solution.py:37
  7.8 10.4 %collective-permute-start = (bf16[1,4,32,256]{3,2,1,0:T(8,128)(2,1)S(1)}, bf16[1,4,32,256]{3,2,1,0:T(8,128)(2,1)S(1)}, u32[]{:S(2)}, u32[]{:S(2)}) collective-permute-start(bf16[1,4,32,256]{3,2,1,0:T(8,128)(2,1)S(1)} %get-tuple-element.44), channel_id=1, source_target_pairs={{0,8},{8,16},{16,24},{24,0},{1,9},{9,17},{17,25},{25,1},{2,10},{10... | collective-permute-start | bytes 196616 | tf_op jit(solution)/shard_map/ppermute | solution.py:36
  8.7 3.9 collective-permute-start.5
  12.6 5.0 %collective-permute-start.6 = (bf16[4,1,32,64]{3,2,0,1:T(8,128)(2,1)S(1)}, bf16[4,1,32,64]{3,2,0,1:T(8,128)(2,1)S(1)}, u32[]{:S(2)}, u32[]{:S(2)}) collective-permute-start(bf16[4,1,32,64]{3,2,0,1:T(8,128)(2,1)S(1)} %bitcast.563), channel_id=1, source_target_pairs={{0,4},{1,5},{2,6},{3,7},{4,0},{5,1},{6,2},{7,3},{8,12},{9,13},{10,... | collective-permute-start | bytes 49160 | tf_op jit(solution)/shard_map/ppermute | solution.py:22
  18.2 7.1 %collective-permute-start.3 = (bf16[4,1,32,256]{3,2,1,0:T(8,128)(2,1)S(1)}, bf16[4,1,32,256]{3,2,1,0:T(8,128)(2,1)S(1)}, u32[]{:S(2)}, u32[]{:S(2)}) collective-permute-start(bf16[4,1,32,256]{3,2,1,0:T(8,128)(2,1)S(1)} %get-tuple-element.36), channel_id=1, source_target_pairs={{1,0},{2,1},{3,2},{4,3},{5,4},{6,5},{7,6},{0,7},{9,8},{10,9},{11,1... | collective-permute-start | bytes 196616 | tf_op jit(solution)/shard_map/ppermute | solution.py:37
  23.4 7.0 %collective-permute-start.2 = (bf16[4,1,32,256]{3,2,1,0:T(8,128)(2,1)S(1)}, bf16[4,1,32,256]{3,2,1,0:T(8,128)(2,1)S(1)}, u32[]{:S(2)}, u32[]{:S(2)}) collective-permute-start(bf16[4,1,32,256]{3,2,1,0:T(8,128)(2,1)S(1)} %get-tuple-element.37), channel_id=1, source_target_pairs={{0,1},{1,2},{2,3},{3,4},{4,5},{5,6},{6,7},{7,0},{8,9},{9,10},{10,1... | collective-permute-start | bytes 196616 | tf_op jit(solution)/shard_map/ppermute | solution.py:36
  30.6 5.4 %copy-start.3 = (f32[1,1,8,256]{3,2,1,0:T(8,128)S(1)}, f32[1,1,8,256]{3,2,1,0:T(8,128)}, u32[]{:S(2)}) copy-start(f32[1,1,8,256]{3,2,1,0:T(8,128)} %param.8) | copy-start | bytes 24580
  121.8 4.0 collective-permute-start.11
  125.8 3.8 collective-permute-start.12
  129.7 4.9 %collective-permute-start.13 = (bf16[4,1,32,64]{3,2,0,1:T(8,128)(2,1)S(1)}, bf16[4,1,32,64]{3,2,0,1:T(8,128)(2,1)S(1)}, u32[]{:S(2)}, u32[]{:S(2)}) collective-permute-start(bf16[4,1,32,64]{3,2,0,1:T(8,128)(2,1)S(1)} %bitcast.565), channel_id=1, source_target_pairs={{0,4},{1,5},{2,6},{3,7},{4,0},{5,1},{6,2},{7,3},{8,12},{9,13},{10,... | collective-permute-start | bytes 49160 | tf_op jit(solution)/shard_map/ppermute | solution.py:22
  129.8 5.3 %collective-permute-start.8 = (bf16[1,4,32,256]{3,2,1,0:T(8,128)(2,1)S(1)}, bf16[1,4,32,256]{3,2,1,0:T(8,128)(2,1)S(1)}, u32[]{:S(2)}, u32[]{:S(2)}) collective-permute-start(bf16[1,4,32,256]{3,2,1,0:T(8,128)(2,1)S(1)} %get-tuple-element.43), channel_id=1, source_target_pairs={{8,0},{16,8},{24,16},{0,24},{9,1},{17,9},{25,17},{1,25},{10,2},{18... | collective-permute-start | bytes 196616 | tf_op jit(solution)/shard_map/ppermute | solution.py:37
  129.9 5.3 %collective-permute-start.7 = (bf16[1,4,32,256]{3,2,1,0:T(8,128)(2,1)S(1)}, bf16[1,4,32,256]{3,2,1,0:T(8,128)(2,1)S(1)}, u32[]{:S(2)}, u32[]{:S(2)}) collective-permute-start(bf16[1,4,32,256]{3,2,1,0:T(8,128)(2,1)S(1)} %get-tuple-element.42), channel_id=1, source_target_pairs={{0,8},{8,16},{16,24},{24,0},{1,9},{9,17},{17,25},{25,1},{2,10},{10... | collective-permute-start | bytes 196616 | tf_op jit(solution)/shard_map/ppermute | solution.py:36
  135.2 5.1 %collective-permute-start.10 = (bf16[4,1,32,256]{3,2,1,0:T(8,128)(2,1)S(1)}, bf16[4,1,32,256]{3,2,1,0:T(8,128)(2,1)S(1)}, u32[]{:S(2)}, u32[]{:S(2)}) collective-permute-start(bf16[4,1,32,256]{3,2,1,0:T(8,128)(2,1)S(1)} %get-tuple-element.30), channel_id=1, source_target_pairs={{1,0},{2,1},{3,2},{4,3},{5,4},{6,5},{7,6},{0,7},{9,8},{10,9},{11,1... | collective-permute-start | bytes 196616 | tf_op jit(solution)/shard_map/ppermute | solution.py:37
  138.4 7.0 %collective-permute-start.9 = (bf16[4,1,32,256]{3,2,1,0:T(8,128)(2,1)S(1)}, bf16[4,1,32,256]{3,2,1,0:T(8,128)(2,1)S(1)}, u32[]{:S(2)}, u32[]{:S(2)}) collective-permute-start(bf16[4,1,32,256]{3,2,1,0:T(8,128)(2,1)S(1)} %get-tuple-element.31), channel_id=1, source_target_pairs={{0,1},{1,2},{2,3},{3,4},{4,5},{5,6},{6,7},{7,0},{8,9},{9,10},{10,1... | collective-permute-start | bytes 196616 | tf_op jit(solution)/shard_map/ppermute | solution.py:36
  235.7 4.0 collective-permute-start.18
  239.7 3.8 collective-permute-start.19
  243.5 4.9 %collective-permute-start.20 = (bf16[4,1,32,64]{3,2,0,1:T(8,128)(2,1)S(1)}, bf16[4,1,32,64]{3,2,0,1:T(8,128)(2,1)S(1)}, u32[]{:S(2)}, u32[]{:S(2)}) collective-permute-start(bf16[4,1,32,64]{3,2,0,1:T(8,128)(2,1)S(1)} %bitcast.567), channel_id=1, source_target_pairs={{0,4},{1,5},{2,6},{3,7},{4,0},{5,1},{6,2},{7,3},{8,12},{9,13},{10,... | collective-permute-start | bytes 49160 | tf_op jit(solution)/shard_map/ppermute | solution.py:22
  243.7 5.3 %collective-permute-start.15 = (bf16[1,4,32,256]{3,2,1,0:T(8,128)(2,1)S(1)}, bf16[1,4,32,256]{3,2,1,0:T(8,128)(2,1)S(1)}, u32[]{:S(2)}, u32[]{:S(2)}) collective-permute-start(bf16[1,4,32,256]{3,2,1,0:T(8,128)(2,1)S(1)} %get-tuple-element.41), channel_id=1, source_target_pairs={{8,0},{16,8},{24,16},{0,24},{9,1},{17,9},{25,17},{1,25},{10,2},{18... | collective-permute-start | bytes 196616 | tf_op jit(solution)/shard_map/ppermute | solution.py:37
  243.8 5.3 %collective-permute-start.14 = (bf16[1,4,32,256]{3,2,1,0:T(8,128)(2,1)S(1)}, bf16[1,4,32,256]{3,2,1,0:T(8,128)(2,1)S(1)}, u32[]{:S(2)}, u32[]{:S(2)}) collective-permute-start(bf16[1,4,32,256]{3,2,1,0:T(8,128)(2,1)S(1)} %get-tuple-element.40), channel_id=1, source_target_pairs={{0,8},{8,16},{16,24},{24,0},{1,9},{9,17},{17,25},{25,1},{2,10},{10... | collective-permute-start | bytes 196616 | tf_op jit(solution)/shard_map/ppermute | solution.py:36
  249.1 5.0 %collective-permute-start.17 = (bf16[4,1,32,256]{3,2,1,0:T(8,128)(2,1)S(1)}, bf16[4,1,32,256]{3,2,1,0:T(8,128)(2,1)S(1)}, u32[]{:S(2)}, u32[]{:S(2)}) collective-permute-start(bf16[4,1,32,256]{3,2,1,0:T(8,128)(2,1)S(1)} %get-tuple-element.26), channel_id=1, source_target_pairs={{1,0},{2,1},{3,2},{4,3},{5,4},{6,5},{7,6},{0,7},{9,8},{10,9},{11,1... | collective-permute-start | bytes 196616 | tf_op jit(solution)/shard_map/ppermute | solution.py:37
  252.1 7.0 %collective-permute-start.16 = (bf16[4,1,32,256]{3,2,1,0:T(8,128)(2,1)S(1)}, bf16[4,1,32,256]{3,2,1,0:T(8,128)(2,1)S(1)}, u32[]{:S(2)}, u32[]{:S(2)}) collective-permute-start(bf16[4,1,32,256]{3,2,1,0:T(8,128)(2,1)S(1)} %get-tuple-element.27), channel_id=1, source_target_pairs={{0,1},{1,2},{2,3},{3,4},{4,5},{5,6},{6,7},{7,0},{8,9},{9,10},{10,1... | collective-permute-start | bytes 196616 | tf_op jit(solution)/shard_map/ppermute | solution.py:36
  350.6 4.0 collective-permute-start.25
  354.6 3.8 collective-permute-start.26
  358.4 4.9 %collective-permute-start.27 = (bf16[4,1,32,64]{3,2,0,1:T(8,128)(2,1)S(1)}, bf16[4,1,32,64]{3,2,0,1:T(8,128)(2,1)S(1)}, u32[]{:S(2)}, u32[]{:S(2)}) collective-permute-start(bf16[4,1,32,64]{3,2,0,1:T(8,128)(2,1)S(1)} %bitcast.561), channel_id=1, source_target_pairs={{0,4},{1,5},{2,6},{3,7},{4,0},{5,1},{6,2},{7,3},{8,12},{9,13},{10,... | collective-permute-start | bytes 49160 | tf_op jit(solution)/shard_map/ppermute | solution.py:22
  358.6 5.3 %collective-permute-start.22 = (bf16[1,4,32,256]{3,2,1,0:T(8,128)(2,1)S(1)}, bf16[1,4,32,256]{3,2,1,0:T(8,128)(2,1)S(1)}, u32[]{:S(2)}, u32[]{:S(2)}) collective-permute-start(bf16[1,4,32,256]{3,2,1,0:T(8,128)(2,1)S(1)} %get-tuple-element.39), channel_id=1, source_target_pairs={{8,0},{16,8},{24,16},{0,24},{9,1},{17,9},{25,17},{1,25},{10,2},{18... | collective-permute-start | bytes 196616 | tf_op jit(solution)/shard_map/ppermute | solution.py:37
  358.7 5.3 %collective-permute-start.21 = (bf16[1,4,32,256]{3,2,1,0:T(8,128)(2,1)S(1)}, bf16[1,4,32,256]{3,2,1,0:T(8,128)(2,1)S(1)}, u32[]{:S(2)}, u32[]{:S(2)}) collective-permute-start(bf16[1,4,32,256]{3,2,1,0:T(8,128)(2,1)S(1)} %get-tuple-element.38), channel_id=1, source_target_pairs={{0,8},{8,16},{16,24},{24,0},{1,9},{9,17},{17,25},{25,1},{2,10},{10... | collective-permute-start | bytes 196616 | tf_op jit(solution)/shard_map/ppermute | solution.py:36
  364.0 5.0 %collective-permute-start.24 = (bf16[4,1,32,256]{3,2,1,0:T(8,128)(2,1)S(1)}, bf16[4,1,32,256]{3,2,1,0:T(8,128)(2,1)S(1)}, u32[]{:S(2)}, u32[]{:S(2)}) collective-permute-start(bf16[4,1,32,256]{3,2,1,0:T(8,128)(2,1)S(1)} %get-tuple-element.22), channel_id=1, source_target_pairs={{1,0},{2,1},{3,2},{4,3},{5,4},{6,5},{7,6},{0,7},{9,8},{10,9},{11,1... | collective-permute-start | bytes 196616 | tf_op jit(solution)/shard_map/ppermute | solution.py:37
  367.1 7.0 %collective-permute-start.23 = (bf16[4,1,32,256]{3,2,1,0:T(8,128)(2,1)S(1)}, bf16[4,1,32,256]{3,2,1,0:T(8,128)(2,1)S(1)}, u32[]{:S(2)}, u32[]{:S(2)}) collective-permute-start(bf16[4,1,32,256]{3,2,1,0:T(8,128)(2,1)S(1)} %get-tuple-element.23), channel_id=1, source_target_pairs={{0,1},{1,2},{2,3},{3,4},{4,5},{5,6},{6,7},{7,0},{8,9},{9,10},{10,1... | collective-permute-start | bytes 196616 | tf_op jit(solution)/shard_map/ppermute | solution.py:36
  (1 other events, 3.2 us)
